TPU v7x, 32 devices: a whole 2x2x4 slice. The times are simulated.
32 devices in a mesh: groups: 2 (over x), tensor: 4 (over y, core), dp: 4 (over z).
Axes of the slice: x: 2, y: 2, z: 4, core: 2. Of those that a mesh axis runs over, the one named last changes fastest.
Arguments:
- hidden_in: bfloat16 [1024, 8192], P(('groups', 'dp'), 'tensor'), parts along dimension 0, may hold values from -6 to 6
- out_grad: bfloat16 [1024, 8192], P(('groups', 'dp'), 'tensor'), parts along dimension 0, may hold values from -6 to 6
- w_gate_up: bfloat16 [2, 28672, 8192], P(None, ('tensor', 'dp')), may hold values from -0.0625 to 0.0625
- w_down: bfloat16 [28672, 8192], P(('tensor', 'dp')), may hold values from -0.03125 to 0.03125
- feat_proj: bfloat16 [8192, 192], P('tensor'), may hold values from -0.0625 to 0.0625
- unit_proj: bfloat16 [28672, 192], P(('tensor', 'dp')), may hold values from -0.03125 to 0.03125
- precond: float32 [3, 4096, 4096], P(None, ('tensor', 'dp')), may hold values from -20 to 20
Outputs:
- precond_grad: float32 [3, 8, 4096], P(None, 'groups', ('tensor', 'dp')), parts along dimension 1
There are 2 independent parts, one for each index of `groups`. A program takes and returns all parts, laid end to end along the dimension named above; an argument that names none is the same for every part. Nothing has to cross between parts.
All inputs are finite; a program needn't handle non-finite values.
Results may differ from a plain program's by a relative error of at most 0.0029.
Values may be sent and summed in bfloat16 or wider, within the bound.
No kernel may reach another device: no remote copies, remote signals or barrier semaphores. Data moves between devices by JAX's collectives and lax.ppermute only.
A program may use at most 256 MiB of HBM per device.

v0:
```python
import jax
import jax.numpy as jnp
from jax import lax
from jax.sharding import PartitionSpec as P

K = 64
SEQ = 128
contract_last = (((1,), (1,)), ((), ()))


def project_pair(rows_in, rows_out, columns):
    return jnp.concatenate(
        [
            jnp.dot(rows_in, columns[:, : 2 * K], preferred_element_type=jnp.float32),
            jnp.dot(rows_out, columns[:, 2 * K :], preferred_element_type=jnp.float32),
        ],
        axis=1,
    )


def form_sketch(in_side, out_side):
    seq_count = in_side.shape[0] // SEQ
    left_rows = in_side.reshape(seq_count, SEQ, 3, K)
    right_rows = out_side.reshape(seq_count, SEQ, 3, K)
    sketch = jnp.einsum("stwi,stwj->wsij", left_rows, right_rows, precision=lax.Precision.HIGHEST)
    sketch = sketch * SEQ ** (-0.5)
    return sketch.reshape(3, seq_count, K * K)


def local(hidden_in, out_grad, w_gate_up, w_down, feat_proj, unit_proj, precond):
    unit_width = w_down.shape[0]
    model_width = w_down.shape[1]
    w_both = w_gate_up.reshape(2 * unit_width, model_width)
    paired = jnp.stack([hidden_in, out_grad])
    tokens = hidden_in.shape[0] * lax.axis_size("dp")
    columns = lax.all_gather(feat_proj, "tensor", axis=0, tiled=True)
    feat_side = None
    rows_all = lax.all_gather(paired, "dp", axis=1, tiled=True)
    initial = [
        jnp.zeros((tokens, 2 * unit_width), jnp.float32),
        jnp.zeros((tokens, unit_width), jnp.float32),
    ]
    initial.append(jnp.zeros((tokens, 3 * K), jnp.float32))
    pieces = lax.all_gather(rows_all, "tensor", axis=2, tiled=True)
    result = [
        lax.dot_general(pieces[0], w_both, contract_last, preferred_element_type=jnp.float32),
        lax.dot_general(pieces[1], w_down, contract_last, preferred_element_type=jnp.float32),
    ]
    result.append(project_pair(pieces[0], pieces[1], columns))
    folded = tuple(result)
    pre_act = folded[0]
    hid_grad = folded[1]
    feat_side = folded[2]
    gate_pre = pre_act[:, :unit_width]
    up_pre = pre_act[:, unit_width:]
    gate_sig = jax.nn.sigmoid(gate_pre)
    silu_gate = gate_pre * gate_sig
    hidden = (silu_gate * up_pre).astype(jnp.bfloat16)
    gate_grad = (hid_grad * up_pre * gate_sig * (1.0 + gate_pre * (1.0 - gate_sig))).astype(
        jnp.bfloat16
    )
    up_grad = (hid_grad * silu_gate).astype(jnp.bfloat16)
    unit_part = jnp.concatenate(
        [
            jnp.dot(gate_grad, unit_proj[:, :K], preferred_element_type=jnp.float32),
            jnp.dot(up_grad, unit_proj[:, K : 2 * K], preferred_element_type=jnp.float32),
            jnp.dot(hidden, unit_proj[:, 2 * K :], preferred_element_type=jnp.float32),
        ],
        axis=1,
    )
    unit_side = lax.psum(unit_part, ("tensor", "dp"))
    in_side = jnp.concatenate([feat_side[:, : 2 * K], unit_side[:, 2 * K :]], axis=1)
    out_side = jnp.concatenate([unit_side[:, : 2 * K], feat_side[:, 2 * K :]], axis=1)
    sketch = form_sketch(in_side, out_side)
    return jnp.einsum("wrc,wsc->wsr", precond, sketch, precision=lax.Precision.HIGHEST)


def solution(mesh):
    in_specs = (
        P(("groups", "dp"), "tensor"),
        P(("groups", "dp"), "tensor"),
        P(None, ("tensor", "dp"), None),
        P(("tensor", "dp"), None),
        P("tensor", None),
        P(("tensor", "dp"), None),
        P(None, ("tensor", "dp"), None),
    )
    out_specs = P(None, "groups", ("tensor", "dp"))
    return jax.shard_map(local, mesh=mesh, in_specs=in_specs, out_specs=out_specs, check_vma=False)
```

profile of v0, /device:TPU:0, one launch (start us, length us, event | category | flops | bytes accessed | tf_op | source)
XLA Modules:
  0.0 386.8 jit_solution(336281864798562320)
XLA Ops:
  6.5 2.3 pad_maximum_fusion
  8.8 0.0 all-gather.6.cloned.1.call-start
  8.9 83.6 %all-gather.4.cloned.1.call-done = bf16[2,512,2048]{2,1,0:T(8,128)(2,1)} async-done(((bf16[2,128,2048]{2,1,0:T(8,128)(2,1)}), bf16[2,512,2048]{2,1,0:T(8,128)(2,1)}) %all-gather.4.cloned.1.call-update) | async-done | bytes 4194320 | tf_op jit(solution)/shard_map/all_gather | solution.py:38
  92.5 0.7 all-gather.8.cloned.1.call-update
  93.2 0.0 all-reduce.2.cloned.1.call-start
  93.3 105.2 %all-gather.6.cloned.1.call-done = bf16[2,512,8192]{2,1,0:T(8,128)(2,1)} async-done(((bf16[2,512,2048]{2,1,0:T(8,128)(2,1)}), bf16[2,512,8192]{2,1,0:T(8,128)(2,1)}) %all-gather.6.cloned.1.call-update) | async-done | bytes 16777232 | tf_op jit(solution)/shard_map/all_gather | solution.py:44
  198.5 38.6 %fusion = f32[512,3584]{1,0:T(8,128)} fusion(bf16[3584,8192]{1,0:T(8,128)(2,1)} %bitcast.23, bf16[2,512,8192]{2,1,0:T(8,128)(2,1)} %all-gather.6.cloned.1.call-done), kind=kOutput, calls=%fused_computation.2 | convolution fusion | flops 30064771072 | bytes 74448896 | tf_op jit(solution)/shard_map/dot_general | solution.py:46
  237.1 4.3 %fusion.7 = f32[512,64]{0,1:T(8,128)S(1)} fusion(f32[512,3584]{1,0:T(8,128)} %fusion, bf16[1792,192]{0,1:T(8,128)(2,1)S(1)} %copy-done), kind=kOutput, calls=%fused_computation.13 | convolution fusion | flops 122945536 | bytes 7700480 | tf_op jit(solution)/shard_map/dot_general | solution.py:67
  241.3 22.9 %fusion.3 = f32[512,1792]{1,0:T(8,128)} fusion(bf16[1792,8192]{1,0:T(8,128)(2,1)} %param.10, bf16[2,512,8192]{2,1,0:T(8,128)(2,1)} %all-gather.6.cloned.1.call-done), kind=kOutput, calls=%fused_computation.5 | convolution fusion | flops 15032385536 | bytes 41418752 | tf_op jit(solution)/shard_map/dot_general | solution.py:47
  264.3 4.4 %fusion.6 = f32[512,64]{0,1:T(8,128)S(1)} fusion(f32[512,1792]{1,0:T(8,128)} %fusion.3, f32[512,3584]{1,0:T(8,128)} %fusion, bf16[1792,192]{0,1:T(8,128)(2,1)S(1)} %copy-done), kind=kOutput, calls=%fused_computation.12 | convolution fusion | flops 122945536 | bytes 7700480 | tf_op jit(solution)/shard_map/dot_general | solution.py:66
  268.7 0.8 copy-done.1
  269.5 1.0 copy-done.2
  270.5 1.6 fusion.8
  272.1 0.8 pad_maximum_fusion.1
  272.9 6.9 %fusion.1 = f32[512,128]{0,1:T(8,128)S(1)} fusion(bf16[2,512,8192]{2,1,0:T(8,128)(2,1)} %all-gather.6.cloned.1.call-done, bf16[8192,192]{0,1:T(8,128)(2,1)} %all-gather.8.cloned.1.call-done), kind=kOutput, calls=%fused_computation.3 | convolution fusion | flops 1073741824 | bytes 10747904 | tf_op jit(solution)/shard_map/dot_general | solution.py:14
  279.8 6.3 %fusion.2 = f32[512,64]{0,1:T(8,128)S(1)} fusion(bf16[2,512,8192]{2,1,0:T(8,128)(2,1)} %all-gather.6.cloned.1.call-done, bf16[8192,192]{0,1:T(8,128)(2,1)} %all-gather.8.cloned.1.call-done), kind=kOutput, calls=%fused_computation.4 | convolution fusion | flops 536870912 | bytes 9568256 | tf_op jit(solution)/shard_map/dot_general | solution.py:15
  286.1 77.3 %all-reduce.2.cloned.1.call-done = f32[512,192]{0,1:T(8,128)} async-done(((f32[512,192]{0,1:T(8,128)}), f32[512,192]{0,1:T(8,128)}) %all-reduce.2.cloned.1.call-update) | async-done | bytes 393232 | tf_op jit(solution)/shard_map/psum | solution.py:71
  363.4 0.9 slice.51
  364.4 0.1 reshape.13
  364.5 1.0 slice.52
  365.5 0.1 reshape.14
  365.7 0.8 convolution_multiply_fusion
  366.4 0.2 reshape.15
  366.6 13.6 %fusion.20 = f32[3,4,256]{2,1,0:T(4,128)} fusion(f32[3,4,4096]{2,1,0:T(4,128)S(1)} %reshape.15, f32[3,256,4096]{2,1,0:T(8,128)} %param.13), kind=kOutput, calls=%fused_computation.29 | convolution fusion | flops 150994944 | bytes 12791808 | tf_op jit(solution)/shard_map/wrc,wsc->wsr/dot_general | solution.py:75
  (12 shorter events, 0.2 us)
Async XLA Ops:
  6.5 85.9 %all-gather.4.cloned.1.call-start = ((), (), s32[]{:S(2)}) async-start(), calls=%async_computation | async-start | bytes 5242880 | tf_op jit(solution)/shard_map/all_gather | solution.py:38
  8.8 189.7 %all-gather.6.cloned.1.call-start = ((), (), s32[]{:S(2)}) async-start(), calls=%async_computation.1 | async-start | bytes 20971520 | tf_op jit(solution)/shard_map/all_gather | solution.py:44
  92.5 180.4 %all-gather.8.cloned.1.call-start = ((), (), s32[]{:S(2)}) async-start(), calls=%async_computation.2 | async-start | bytes 3932160 | tf_op jit(solution)/shard_map/all_gather | solution.py:36
  93.2 270.2 %all-reduce.2.cloned.1.call-start = ((), (), s32[]{:S(2)}) async-start(), calls=%async_computation.3 | async-start | bytes 786432 | tf_op jit(solution)/shard_map/psum | solution.py:71
  198.5 38.6 %copy-start = (bf16[1792,192]{0,1:T(8,128)(2,1)S(1)}, bf16[1792,192]{0,1:T(8,128)(2,1)}, u32[]{:S(2)}) copy-start(bf16[1792,192]{0,1:T(8,128)(2,1)} %param.12) | copy-start | bytes 2064388
  264.3 5.2 %copy-start.1 = (f32[512,3584]{1,0:T(8,128)S(1)}, f32[512,3584]{1,0:T(8,128)}, u32[]{:S(2)}) copy-start(f32[512,3584]{1,0:T(8,128)} %fusion) | copy-start | bytes 22020100
  264.3 6.3 %copy-start.2 = (f32[512,1792]{1,0:T(8,128)S(1)}, f32[512,1792]{1,0:T(8,128)}, u32[]{:S(2)}) copy-start(f32[512,1792]{1,0:T(8,128)} %fusion.3) | copy-start | bytes 11010052
Sparse Core Ops, SparseCore 0:
  9.0 83.4 all-gather.3
  94.0 104.4 all-gather.5
  200.1 28.5 all-gather.7
  273.0 90.3 all-reduce.1
where the time goes:
time: 387 us
  waiting for transfers between devices  267 us (69%)
  matrix products  99.3 us (26%)
  between operations  13.2 us (3%)
  local copies, waits for them, and re-layouts  4.2 us (1%)
    all_gather x1, waiting for transfers between devices, local(): pieces = lax.all_gather(rows_all, 'tensor', axis=2, tiled=True)  105 us
    all_gather x1, waiting for transfers between devices, local(): rows_all = lax.all_gather(paired, 'dp', axis=1, tiled=True)  83.6 us
    psum x1, waiting for transfers between devices, local(): unit_side = lax.psum(unit_part, ('tensor', 'dp'))  77.3 us
    dot_general x1, matrix products, local(): lax.dot_general(pieces[0], w_both, contract_last, preferred_element_type=...  38.6 us
    dot_general x1, matrix products, local(): lax.dot_general(pieces[1], w_down, contract_last, preferred_element_type=...  22.9 us
    dot_general x1, matrix products, local(): jnp.einsum('wrc,wsc->wsr', precond, sketch, precision=lax.Precision.HIGHEST)  13.6 us
  transfers between devices with their start and end apart: 4, of which 3 were waited for; matrix products, arithmetic and copies ran while one was open for 22% of the time, Pallas kernels for 0%

commit v1 on v0

--- a/solution.py
+++ b/solution.py
@@ -41,7 +41,16 @@
         jnp.zeros((tokens, unit_width), jnp.float32),
     ]
     initial.append(jnp.zeros((tokens, 3 * K), jnp.float32))
-    pieces = lax.all_gather(rows_all, "tensor", axis=2, tiled=True)
+    row_out, part_next = (lax.axis_size("tensor"), lax.axis_index("tensor"))
+    pieces, z_new = (rows_all, 1)
+    while z_new < row_out:
+        side_arr = lax.ppermute(
+            pieces, axis_name="tensor", perm=[(b, b ^ z_new) for b in range(row_out)]
+        )
+        found_now = jnp.concatenate([pieces, side_arr], 2)
+        later = jnp.concatenate([side_arr, pieces], axis=2)
+        pieces = jnp.where(part_next & z_new == 0, found_now, later)
+        z_new = 2 * z_new
     result = [
         lax.dot_general(pieces[0], w_both, contract_last, preferred_element_type=jnp.float32),
         lax.dot_general(pieces[1], w_down, contract_last, preferred_element_type=jnp.float32),

time: 387 us -> 519 us (1.34)
  waiting for transfers between devices: 267 us -> 365 us
  other arithmetic: 3.1 us -> 33.6 us
    ppermute x0 -> x2, waiting for transfers between devices: none -> 206 us  [local(): lax.ppermute(pieces, axis_name='tensor', perm=[(b, b ^ z_new) for b in ra...]
    all_gather x1 -> x0, waiting for transfers between devices: 105 us -> none  [local(): pieces = lax.all_gather(rows_all, 'tensor', axis=2, tiled=True)]
    select_n x0 -> x2, other arithmetic: none -> 30.5 us  [local(): pieces = jnp.where(part_next & z_new == 0, found_now, later)]
  transfers between devices with their start and end apart: 4 -> 5, of which waited for: 3 -> 4; matrix products, arithmetic and copies ran while one was open for 22% -> 20% of each run, Pallas kernels for 0% -> 0%
where the time goes in v1:
time: 519 us
  waiting for transfers between devices  365 us (70%)
  matrix products  99.3 us (19%)
  other arithmetic  33.6 us (6%)
  between operations  14.9 us (3%)
    ppermute x2, waiting for transfers between devices, local(): lax.ppermute(pieces, axis_name='tensor', perm=[(b, b ^ z_new) for b in ra...  206 us
    all_gather x1, waiting for transfers between devices, local(): rows_all = lax.all_gather(paired, 'dp', axis=1, tiled=True)  83.6 us
    psum x1, waiting for transfers between devices, local(): unit_side = lax.psum(unit_part, ('tensor', 'dp'))  75.8 us
    dot_general x1, matrix products, local(): lax.dot_general(pieces[0], w_both, contract_last, preferred_element_type=...  38.6 us
    select_n x2, other arithmetic, local(): pieces = jnp.where(part_next & z_new == 0, found_now, later)  30.5 us
    dot_general x1, matrix products, local(): lax.dot_general(pieces[1], w_down, contract_last, preferred_element_type=...  22.9 us
    dot_general x1, matrix products, local(): jnp.einsum('wrc,wsc->wsr', precond, sketch, precision=lax.Precision.HIGHEST)  13.6 us
  transfers between devices with their start and end apart: 5, of which 4 were waited for; matrix products, arithmetic and copies ran while one was open for 20% of the time, Pallas kernels for 0%

profile of v1, /device:TPU:0, one launch (start us, length us, event | category | flops | bytes accessed | tf_op | source)
XLA Modules:
  0.0 518.6 jit_solution(16318961568072994263)
XLA Ops:
  7.4 2.3 pad_maximum_fusion
  9.7 83.6 %all-gather.3.cloned.1.call-done = bf16[2,512,2048]{2,1,0:T(8,128)(2,1)} async-done(((bf16[2,128,2048]{2,1,0:T(8,128)(2,1)}), bf16[2,512,2048]{2,1,0:T(8,128)(2,1)}) %all-gather.3.cloned.1.call-update) | async-done | bytes 4194320 | tf_op jit(solution)/shard_map/all_gather | solution.py:38
  93.3 7.5 %collective-permute-done = bf16[2,512,2048]{2,1,0:T(8,128)(2,1)} collective-permute-done((bf16[2,512,2048]{2,1,0:T(8,128)(2,1)}, bf16[2,512,2048]{2,1,0:T(8,128)(2,1)}, u32[]{:S(2)}, u32[]{:S(2)}) %collective-permute-start) | collective-permute-done | bytes 4194336 | tf_op jit(solution)/shard_map/ppermute | solution.py:47
  100.8 11.3 %maximum_select_fusion.1 = bf16[2,512,4096]{2,1,0:T(8,128)(2,1)} fusion(bf16[2,512,2048]{2,1,0:T(8,128)(2,1)} %collective-permute-done, bf16[2,512,2048]{2,1,0:T(8,128)(2,1)} %all-gather.3.cloned.1.call-done, pred[]{:T(512)S(6)} %eq.7), kind=kLoop, calls=%fused_computation.3 | loop fusion | flops 37748736 | bytes 16777216 | tf_op jit(solution)/shard_map/jit(_where)/select_n | solution.py:52
  112.1 1.5 collective-permute-start.1
  113.6 198.1 %collective-permute-done.1 = bf16[2,512,4096]{2,1,0:T(8,128)(2,1)} collective-permute-done((bf16[2,512,4096]{2,1,0:T(8,128)(2,1)}, bf16[2,512,4096]{2,1,0:T(8,128)(2,1)}, u32[]{:S(2)}, u32[]{:S(2)}) %collective-permute-start.1) | collective-permute-done | bytes 8388640 | tf_op jit(solution)/shard_map/ppermute | solution.py:47
  311.7 19.2 %maximum_select_fusion = bf16[2,512,8192]{2,1,0:T(8,128)(2,1)} fusion(bf16[2,512,4096]{2,1,0:T(8,128)(2,1)} %collective-permute-done.1, bf16[2,512,4096]{2,1,0:T(8,128)(2,1)} %maximum_select_fusion.1, pred[]{:T(512)S(6)} %eq.6), kind=kLoop, calls=%fused_computation | loop fusion | flops 75497472 | bytes 33554432 | tf_op jit(solution)/shard_map/jit(_where)/select_n | solution.py:52
  330.9 38.6 %fusion = f32[512,3584]{1,0:T(8,128)} fusion(bf16[3584,8192]{1,0:T(8,128)(2,1)} %bitcast.23, bf16[2,512,8192]{2,1,0:T(8,128)(2,1)} %maximum_select_fusion), kind=kOutput, calls=%fused_computation.4 | convolution fusion | flops 30064771072 | bytes 74448896 | tf_op jit(solution)/shard_map/dot_general | solution.py:55
  369.5 4.3 fusion.7
  373.8 22.9 %fusion.3 = f32[512,1792]{1,0:T(8,128)} fusion(bf16[1792,8192]{1,0:T(8,128)(2,1)} %param.10, bf16[2,512,8192]{2,1,0:T(8,128)(2,1)} %maximum_select_fusion), kind=kOutput, calls=%fused_computation.7 | convolution fusion | flops 15032385536 | bytes 41418752 | tf_op jit(solution)/shard_map/dot_general | solution.py:56
  396.7 4.4 fusion.6
  401.1 0.8 copy-done.1
  401.9 1.0 copy-done.2
  402.9 1.6 fusion.8
  404.5 0.8 pad_maximum_fusion.1
  405.3 6.9 %fusion.1 = f32[512,128]{0,1:T(8,128)S(1)} fusion(bf16[2,512,8192]{2,1,0:T(8,128)(2,1)} %maximum_select_fusion, bf16[8192,192]{0,1:T(8,128)(2,1)} %all-gather.5.cloned.1.call-done), kind=kOutput, calls=%fused_computation.5 | convolution fusion | flops 1073741824 | bytes 10747904 | tf_op jit(solution)/shard_map/dot_general | solution.py:14
  412.2 6.3 %fusion.2 = f32[512,64]{0,1:T(8,128)S(1)} fusion(bf16[2,512,8192]{2,1,0:T(8,128)(2,1)} %maximum_select_fusion, bf16[8192,192]{0,1:T(8,128)(2,1)} %all-gather.5.cloned.1.call-done), kind=kOutput, calls=%fused_computation.6 | convolution fusion | flops 536870912 | bytes 9568256 | tf_op jit(solution)/shard_map/dot_general | solution.py:15
  418.5 75.8 %all-reduce.2.cloned.1.call-done = f32[512,192]{0,1:T(8,128)} async-done(((f32[512,192]{0,1:T(8,128)}), f32[512,192]{0,1:T(8,128)}) %all-reduce.2.cloned.1.call-update) | async-done | bytes 393232 | tf_op jit(solution)/shard_map/psum | solution.py:80
  494.4 0.9 slice.51
  495.3 0.1 reshape.13
  495.5 1.0 slice.52
  496.6 0.7 convolution_multiply_fusion
  497.4 0.2 reshape.15
  497.6 13.6 %fusion.20 = f32[3,4,256]{2,1,0:T(4,128)} fusion(f32[3,4,4096]{2,1,0:T(4,128)S(1)} %reshape.15, f32[3,256,4096]{2,1,0:T(8,128)} %param.13), kind=kOutput, calls=%fused_computation.31 | convolution fusion | flops 150994944 | bytes 12791808 | tf_op jit(solution)/shard_map/wrc,wsc->wsr/dot_general | solution.py:84
  (15 shorter events, 0.4 us)
Async XLA Ops:
  7.4 85.9 %all-gather.3.cloned.1.call-start = ((), (), s32[]{:S(2)}) async-start(), calls=%async_computation | async-start | bytes 5242880 | tf_op jit(solution)/shard_map/all_gather | solution.py:38
  9.7 395.7 %all-gather.5.cloned.1.call-start = ((), (), s32[]{:S(2)}) async-start(), calls=%async_computation.1 | async-start | bytes 3932160 | tf_op jit(solution)/shard_map/all_gather | solution.py:36
  93.3 7.5 %collective-permute-start = (bf16[2,512,2048]{2,1,0:T(8,128)(2,1)}, bf16[2,512,2048]{2,1,0:T(8,128)(2,1)}, u32[]{:S(2)}, u32[]{:S(2)}) collective-permute-start(bf16[2,512,2048]{2,1,0:T(8,128)(2,1)} %all-gather.3.cloned.1.call-done), channel_id=1, source_target_pairs={{0,4},{4,0},{8,12},{12,8},{1,5},{5,1},{9,13},{13,9},{2,6},{6,2},{1... | collective-permute-start | bytes 12582920 | tf_op jit(solution)/shard_map/ppermute | solution.py:47
  112.1 199.7 %collective-permute-start.1 = (bf16[2,512,4096]{2,1,0:T(8,128)(2,1)}, bf16[2,512,4096]{2,1,0:T(8,128)(2,1)}, u32[]{:S(2)}, u32[]{:S(2)}) collective-permute-start(bf16[2,512,4096]{2,1,0:T(8,128)(2,1)} %maximum_select_fusion.1), channel_id=1, source_target_pairs={{0,8},{4,12},{8,0},{12,4},{1,9},{5,13},{9,1},{13,5},{2,10},{6,14},... | collective-permute-start | bytes 25165832 | tf_op jit(solution)/shard_map/ppermute | solution.py:47
  113.6 380.8 %all-reduce.2.cloned.1.call-start = ((), (), s32[]{:S(2)}) async-start(), calls=%async_computation.2 | async-start | bytes 786432 | tf_op jit(solution)/shard_map/psum | solution.py:80
  330.9 38.6 %copy-start = (bf16[1792,192]{0,1:T(8,128)(2,1)S(1)}, bf16[1792,192]{0,1:T(8,128)(2,1)}, u32[]{:S(2)}) copy-start(bf16[1792,192]{0,1:T(8,128)(2,1)} %param.12) | copy-start | bytes 2064388
  396.7 5.2 %copy-start.1 = (f32[512,3584]{1,0:T(8,128)S(1)}, f32[512,3584]{1,0:T(8,128)}, u32[]{:S(2)}) copy-start(f32[512,3584]{1,0:T(8,128)} %fusion) | copy-start | bytes 22020100
  396.7 6.3 %copy-start.2 = (f32[512,1792]{1,0:T(8,128)S(1)}, f32[512,1792]{1,0:T(8,128)}, u32[]{:S(2)}) copy-start(f32[512,1792]{1,0:T(8,128)} %fusion.3) | copy-start | bytes 11010052
Sparse Core Ops, SparseCore 0:
  9.8 83.4 all-gather.2
  405.4 88.8 all-reduce.1
Sparse Core Ops, SparseCore 1:
  113.6 42.9 all-gather.4
